TPU v7x, 256 devices: a whole 4x4x8 slice. The times are simulated.
256 devices in a mesh: chan: 32 (over x_hi, z, core), bfly: 2 (over x_lo), samp: 4 (over y).
Axes of the slice: x: 4 (x_hi: 2, x_lo: 2; x = x_hi * 2 + x_lo), y: 4, z: 8, core: 2. Of those that a mesh axis runs over, the one named last changes fastest.
Arguments:
- features: bfloat16 [65536, 2048], P(('chan', 'bfly'), 'samp'), may hold values from -6 to 6
- cotangent: bfloat16 [65536, 2048], P(('chan', 'bfly'), 'samp'), may hold values from -6 to 6
- right_factor: bfloat16 [2, 256, 256, 256], P(None, ('chan', 'bfly')), may hold values from -0.375 to 0.375
- left_factor: float32 [2, 256, 256, 256], P(None, ('chan', 'bfly')), may hold values from -0.375 to 0.375
- mixing: float32 [2, 2, 256, 256], P(None, None, ('chan', 'bfly')), may hold values from -1.2 to 1.2
Outputs:
- output: bfloat16 [65536, 2048], P(('chan', 'bfly'), 'samp')
- feature_grad: bfloat16 [65536, 2048], P(('chan', 'bfly'), 'samp')
- grad_right: float32 [2, 256, 256, 256], P(None, ('chan', 'bfly'))
- grad_left: float32 [2, 256, 256, 256], P(None, ('chan', 'bfly'))
- grad_mixing: float32 [2, 2, 256, 256], P(None, None, ('chan', 'bfly'))
All inputs are finite; a program needn't handle non-finite values.
Results may differ from a plain program's by a relative error of at most 0.025.
Values may be sent and summed in bfloat16 or wider, within the bound.
A program may use at most 128 MiB of HBM per device.

v0:
```python
import jax
import jax.numpy as jnp
from jax import lax
from jax.sharding import PartitionSpec as P

BLOCK = 256
LAYERS = 2


def partner_2(block, axis, distance):
    count = lax.axis_size(axis)
    route = []
    for low in range(count):
        high = low | 1 << distance
        if high != low and high < count:
            route += [(low, high), (high, low)]
    return lax.ppermute(block, axis, route)


def to_columns(values):
    return lax.all_to_all(values, ("chan", "bfly"), split_axis=1, concat_axis=0, tiled=True)


def to_rows(values):
    return lax.all_to_all(values, ("chan", "bfly"), split_axis=0, concat_axis=1, tiled=True)


def local(features, cotangent, right_factor, left_factor, mixing):
    blocks = right_factor.shape[1]
    samples = features.shape[1]
    height = features.reshape(blocks, BLOCK, samples)
    saved = []
    for layer_index in range(LAYERS):
        mixed_u = jnp.einsum(
            "bis,bij->bjs", height, right_factor[layer_index], preferred_element_type=jnp.float32
        ).astype(jnp.bfloat16)
        self_gain = mixing[layer_index, 0][:, :, None]
        cross_gain = mixing[layer_index, 1][:, :, None]
        partner = partner_2(mixed_u, "bfly", 0)
        mixed_v = (self_gain * mixed_u + cross_gain * partner).astype(jnp.bfloat16)
        columns = to_columns(mixed_v)
        kept = (mixed_u, partner)
        outer = jnp.einsum(
            "bjs,jbk->kjs", columns, left_factor[layer_index], preferred_element_type=jnp.float32
        ).astype(jnp.bfloat16)
        activation = to_rows(outer)
        saved.append((height, kept, columns, activation))
        height = (height.astype(jnp.float32) + jax.nn.silu(activation.astype(jnp.float32))).astype(
            jnp.bfloat16
        )
    output = height.reshape(blocks * BLOCK, samples)
    grad = cotangent.reshape(blocks, BLOCK, samples)
    rights = [None] * LAYERS
    lefts = [None] * LAYERS
    mixes = [None] * LAYERS
    for layer_index in reversed(range(LAYERS)):
        height_in, kept, columns, activation = saved[layer_index]
        before = activation.astype(jnp.float32)
        logistic = jax.nn.sigmoid(before)
        error = (grad.astype(jnp.float32) * logistic * (1.0 + before * (1.0 - logistic))).astype(
            jnp.bfloat16
        )
        error_cols = to_columns(error)
        grad_left = jnp.einsum(
            "bjs,kjs->jbk", columns, error_cols, preferred_element_type=jnp.float32
        )
        grad_cols = jnp.einsum(
            "jbk,kjs->bjs", left_factor[layer_index], error_cols, preferred_element_type=jnp.float32
        ).astype(jnp.bfloat16)
        mixed_u, partner = kept
        self_gain = mixing[layer_index, 0][:, :, None]
        cross_gain = mixing[layer_index, 1][:, :, None]
        grad_v = to_rows(grad_cols)
        grad_mix = jnp.stack(
            [
                jnp.einsum("bjs,bjs->bj", grad_v, mixed_u, preferred_element_type=jnp.float32),
                jnp.einsum("bjs,bjs->bj", grad_v, partner, preferred_element_type=jnp.float32),
            ]
        )
        carried = (cross_gain * grad_v).astype(jnp.bfloat16)
        returned = partner_2(carried, "bfly", 0)
        grad_u = (self_gain * grad_v + returned.astype(jnp.float32)).astype(jnp.bfloat16)
        grad_right = jnp.einsum(
            "bis,bjs->bij", height_in, grad_u, preferred_element_type=jnp.float32
        )
        back_term = jnp.einsum(
            "bij,bjs->bis", right_factor[layer_index], grad_u, preferred_element_type=jnp.float32
        )
        grad = (grad.astype(jnp.float32) + back_term).astype(jnp.bfloat16)
        rights[layer_index] = grad_right
        lefts[layer_index] = grad_left
        mixes[layer_index] = grad_mix
    all_right = jnp.stack(rights)
    all_left = jnp.stack(lefts)
    all_mix = jnp.stack(mixes)
    all_right, all_left, all_mix = (
        lax.psum(all_right.astype(jnp.bfloat16), "samp").astype(jnp.float32),
        lax.psum(all_left.astype(jnp.bfloat16), "samp").astype(jnp.float32),
        lax.psum(all_mix.astype(jnp.bfloat16), "samp").astype(jnp.float32),
    )
    return (output, grad.reshape(blocks * BLOCK, samples), all_right, all_left, all_mix)


def solution(mesh):
    in_specs = (
        P(("chan", "bfly"), "samp"),
        P(("chan", "bfly"), "samp"),
        P(None, ("chan", "bfly"), None, None),
        P(None, ("chan", "bfly"), None, None),
        P(None, None, ("chan", "bfly"), None),
    )
    out_specs = (
        P(("chan", "bfly"), "samp"),
        P(("chan", "bfly"), "samp"),
        P(None, ("chan", "bfly"), None, None),
        P(None, ("chan", "bfly"), None, None),
        P(None, None, ("chan", "bfly"), None),
    )
    return jax.shard_map(local, mesh=mesh, in_specs=in_specs, out_specs=out_specs, check_vma=False)
```

profile of v0, /device:TPU:1, one launch (start us, length us, event | category | flops | bytes accessed | tf_op | source)
XLA Modules:
  0.0 527.4 jit_solution(5031912849368408522)
XLA Ops:
  11.2 21.5 %collective-permute-done = bf16[4,256,512]{2,1,0:T(8,128)(2,1)S(1)} collective-permute-done((bf16[4,256,512]{2,1,0:T(8,128)(2,1)S(1)}, bf16[4,256,512]{2,1,0:T(8,128)(2,1)S(1)}, u32[]{:S(2)}, u32[]{:S(2)}) %collective-permute-start) | collective-permute-done | bytes 1048608 | tf_op jit(solution)/shard_map/ppermute | solution.py:17
  34.7 43.4 %all_to_all.126 = bf16[4,256,512]{2,0,1:T(4,128)(2,1)S(1)} all-to-all(bf16[4,256,512]{2,0,1:T(4,128)(2,1)S(1)} %copy.92), channel_id=1, replica_groups=mesh['chan'=32,'bfly'=2,'samp'=4] {'chan','bfly'}, dimensions={1} | all-to-all | bytes 2097152 | tf_op jit(solution)/shard_map/all_to_all | solution.py:21
  82.0 34.5 %all_to_all.127 = bf16[256,4,512]{2,1,0:T(4,128)(2,1)S(1)} all-to-all(bf16[256,4,512]{2,1,0:T(4,128)(2,1)S(1)} %copy.95), channel_id=1, replica_groups=mesh['chan'=32,'bfly'=2,'samp'=4] {'chan','bfly'}, dimensions={0} | all-to-all | bytes 2097152 | tf_op jit(solution)/shard_map/all_to_all | solution.py:25
  123.7 22.6 %collective-permute-done.1 = bf16[4,256,512]{1,2,0:T(8,128)(2,1)S(1)} collective-permute-done((bf16[4,256,512]{1,2,0:T(8,128)(2,1)S(1)}, bf16[4,256,512]{1,2,0:T(8,128)(2,1)S(1)}, u32[]{:S(2)}, u32[]{:S(2)}) %collective-permute-start.1) | collective-permute-done | bytes 1048608 | tf_op jit(solution)/shard_map/ppermute | solution.py:17
  151.3 35.6 %all_to_all.128 = bf16[4,256,512]{2,0,1:T(4,128)(2,1)S(1)} all-to-all(bf16[4,256,512]{2,0,1:T(4,128)(2,1)} %copy.99), channel_id=1, replica_groups=mesh['chan'=32,'bfly'=2,'samp'=4] {'chan','bfly'}, dimensions={1} | all-to-all | bytes 2097152 | tf_op jit(solution)/shard_map/all_to_all | solution.py:21
  192.6 34.7 %all_to_all.129 = bf16[256,4,512]{2,1,0:T(4,128)(2,1)S(1)} all-to-all(bf16[256,4,512]{2,1,0:T(4,128)(2,1)} %copy.102), channel_id=1, replica_groups=mesh['chan'=32,'bfly'=2,'samp'=4] {'chan','bfly'}, dimensions={0} | all-to-all | bytes 2097152 | tf_op jit(solution)/shard_map/all_to_all | solution.py:25
  229.3 2.9 reshape.48
  232.3 2.7 fusion.13
  235.8 34.6 %all_to_all.130 = bf16[4,256,512]{2,0,1:T(4,128)(2,1)S(1)} all-to-all(bf16[4,256,512]{2,0,1:T(4,128)(2,1)S(1)} %copy.105), channel_id=1, replica_groups=mesh['chan'=32,'bfly'=2,'samp'=4] {'chan','bfly'}, dimensions={1} | all-to-all | bytes 2097152 | tf_op jit(solution)/shard_map/all_to_all | solution.py:21
  276.1 34.7 %all_to_all.131 = bf16[256,4,512]{2,1,0:T(4,128)(2,1)S(1)} all-to-all(bf16[256,4,512]{2,1,0:T(4,128)(2,1)} %copy.108), channel_id=1, replica_groups=mesh['chan'=32,'bfly'=2,'samp'=4] {'chan','bfly'}, dimensions={0} | all-to-all | bytes 2097152 | tf_op jit(solution)/shard_map/all_to_all | solution.py:25
  318.2 22.6 %collective-permute-done.2 = bf16[4,256,512]{1,2,0:T(8,128)(2,1)S(1)} collective-permute-done((bf16[4,256,512]{1,2,0:T(8,128)(2,1)S(1)}, bf16[4,256,512]{1,2,0:T(8,128)(2,1)S(1)}, u32[]{:S(2)}, u32[]{:S(2)}) %collective-permute-start.2) | collective-permute-done | bytes 1048608 | tf_op jit(solution)/shard_map/ppermute | solution.py:17
  340.9 4.4 fusion.10
  346.1 35.4 %all_to_all.132 = bf16[4,256,512]{2,0,1:T(4,128)(2,1)S(1)} all-to-all(bf16[4,256,512]{2,0,1:T(4,128)(2,1)S(1)} %copy.112), channel_id=1, replica_groups=mesh['chan'=32,'bfly'=2,'samp'=4] {'chan','bfly'}, dimensions={1} | all-to-all | bytes 2097152 | tf_op jit(solution)/shard_map/all_to_all | solution.py:21
  384.5 2.6 copy.115
  387.1 34.7 %all_to_all.133 = bf16[256,4,512]{2,1,0:T(4,128)(2,1)S(1)} all-to-all(bf16[256,4,512]{2,1,0:T(4,128)(2,1)} %copy.115), channel_id=1, replica_groups=mesh['chan'=32,'bfly'=2,'samp'=4] {'chan','bfly'}, dimensions={0} | all-to-all | bytes 2097152 | tf_op jit(solution)/shard_map/all_to_all | solution.py:25
  425.3 2.8 fusion.18
  433.8 19.0 %collective-permute-done.3 = bf16[4,256,512]{2,1,0:T(8,128)(2,1)S(1)} collective-permute-done((bf16[4,256,512]{2,1,0:T(8,128)(2,1)S(1)}, bf16[4,256,512]{2,1,0:T(8,128)(2,1)S(1)}, u32[]{:S(2)}, u32[]{:S(2)}) %collective-permute-start.3) | collective-permute-done | bytes 1048608 | tf_op jit(solution)/shard_map/ppermute | solution.py:17
  456.7 3.0 reshape.46
  459.7 4.5 add_convert_fusion
  465.9 3.0 copy.141
  471.0 10.0 %psum.23 = bf16[2,2,4,256]{3,2,1,0:T(4,128)(2,1)S(1)} all-reduce(bf16[2,2,4,256]{3,2,1,0:T(4,128)(2,1)S(1)} %pad_maximum_fusion.2), channel_id=1, replica_groups=mesh['chan'=32,'bfly'=2,'samp'=4] {'samp'}, use_global_device_ids=true, to_apply=%region_2.3 | all-reduce | flops 4096 | bytes 16384 | tf_op jit(solution)/shard_map/psum | solution.py:99
  481.7 3.4 fusion.11
  485.0 31.4 %all-reduce.3.cloned.1.call-done = (bf16[2,4,256,256]{2,3,1,0:T(8,128)(2,1)}, bf16[2,4,256,256]{3,2,1,0:T(8,128)(2,1)}) async-done(((bf16[2,4,256,256]{2,3,1,0:T(8,128)(2,1)}, bf16[2,4,256,256]{3,2,1,0:T(8,128)(2,1)}), (bf16[2,4,256,256]{2,3,1,0:T(8,128)(2,1)}, bf16[2,4,256,256]{3,2,1,0:T(8,128)(2,1)})) %all-reduce.3.cloned.1.call-update) | async-done | bytes 2097168 | tf_op jit(solution)/shard_map/psum | solution.py:97
  516.4 2.7 copy.124
  (116 shorter events, 66.5 us)
Async XLA Ops:
  7.2 4.1 copy-start.32
  7.2 509.2 %all-reduce.3.cloned.1.call-start = ((), (), s32[]{:S(2)}) async-start(), calls=%async_computation.8 | async-start | bytes 4194304 | tf_op jit(solution)/shard_map/psum | solution.py:97
  9.1 25.5 %copy-start.1 = (bf16[4,256,512]{2,1,0:T(8,128)(2,1)}, bf16[4,256,512]{2,1,0:T(8,128)(2,1)S(1)}, u32[]{:S(2)}) copy-start(bf16[4,256,512]{2,1,0:T(8,128)(2,1)S(1)} %convolution_convert_fusion.5) | copy-start | bytes 3145732
  9.1 23.7 %collective-permute-start = (bf16[4,256,512]{2,1,0:T(8,128)(2,1)S(1)}, bf16[4,256,512]{2,1,0:T(8,128)(2,1)S(1)}, u32[]{:S(2)}, u32[]{:S(2)}) collective-permute-start(bf16[4,256,512]{2,1,0:T(8,128)(2,1)S(1)} %convolution_convert_fusion.5), channel_id=1, source_target_pairs={{0,4},{4,0},{1,5},{5,1},{2,6},{6,2},{3,7},{7,3},{8,12},{12,8},{9,1... | collective-permute-start | bytes 3145736 | tf_op jit(solution)/shard_map/ppermute | solution.py:17
  34.7 44.0 %copy-start.11 = (f32[2,4,256,256]{3,2,1,0:T(8,128)S(1)}, f32[2,4,256,256]{3,2,1,0:T(8,128)}, u32[]{:S(2)}) copy-start(f32[2,4,256,256]{3,2,1,0:T(8,128)} %param.8) | copy-start | bytes 6291460
  78.6 3.4 copy-start.17
  121.4 24.9 %copy-start.7 = (bf16[4,256,512]{2,1,0:T(8,128)(2,1)}, bf16[4,256,512]{2,1,0:T(8,128)(2,1)S(1)}, u32[]{:S(2)}) copy-start(bf16[4,256,512]{2,1,0:T(8,128)(2,1)S(1)} %add_convert_fusion.1) | copy-start | bytes 3145732
  121.9 24.4 %collective-permute-start.1 = (bf16[4,256,512]{1,2,0:T(8,128)(2,1)S(1)}, bf16[4,256,512]{1,2,0:T(8,128)(2,1)S(1)}, u32[]{:S(2)}, u32[]{:S(2)}) collective-permute-start(bf16[4,256,512]{1,2,0:T(8,128)(2,1)S(1)} %fusion.24), channel_id=1, source_target_pairs={{0,4},{4,0},{1,5},{5,1},{2,6},{6,2},{3,7},{7,3},{8,12},{12,8},{9,1... | collective-permute-start | bytes 3145736 | tf_op jit(solution)/shard_map/ppermute | solution.py:17
  151.3 37.1 %copy-start.12 = (f32[2,4,256,256]{3,2,1,0:T(8,128)S(1)}, f32[2,4,256,256]{3,2,1,0:T(8,128)}, u32[]{:S(2)}) copy-start(f32[2,4,256,256]{3,2,1,0:T(8,128)} %param.8) | copy-start | bytes 6291460
  235.8 36.1 %copy-start.13 = (f32[2,4,256,256]{3,2,1,0:T(8,128)S(1)}, f32[2,4,256,256]{3,2,1,0:T(8,128)}, u32[]{:S(2)}) copy-start(f32[2,4,256,256]{3,2,1,0:T(8,128)} %param.8) | copy-start | bytes 6291460
  314.7 26.2 %copy-start.2 = (bf16[4,256,512]{1,2,0:T(8,128)(2,1)S(1)}, bf16[4,256,512]{1,2,0:T(8,128)(2,1)}, u32[]{:S(2)}) copy-start(bf16[4,256,512]{1,2,0:T(8,128)(2,1)} %copy.110) | copy-start | bytes 3145732
  314.7 26.2 %copy-start.27 = (bf16[2,4,256,256]{3,2,1,0:T(8,128)(2,1)S(1)}, bf16[2,4,256,256]{3,2,1,0:T(8,128)(2,1)}, u32[]{:S(2)}) copy-start(bf16[2,4,256,256]{3,2,1,0:T(8,128)(2,1)} %param.7) | copy-start | bytes 3145732
  316.2 24.6 %collective-permute-start.2 = (bf16[4,256,512]{1,2,0:T(8,128)(2,1)S(1)}, bf16[4,256,512]{1,2,0:T(8,128)(2,1)S(1)}, u32[]{:S(2)}, u32[]{:S(2)}) collective-permute-start(bf16[4,256,512]{1,2,0:T(8,128)(2,1)S(1)} %fusion.8), channel_id=1, source_target_pairs={{0,4},{4,0},{1,5},{5,1},{2,6},{6,2},{3,7},{7,3},{8,12},{12,8},{9,1... | collective-permute-start | bytes 3145736 | tf_op jit(solution)/shard_map/ppermute | solution.py:17
  340.9 4.4 copy-start.30
  346.1 36.9 %copy-start.14 = (f32[2,4,256,256]{3,2,1,0:T(8,128)S(1)}, f32[2,4,256,256]{3,2,1,0:T(8,128)}, u32[]{:S(2)}) copy-start(f32[2,4,256,256]{3,2,1,0:T(8,128)} %param.8) | copy-start | bytes 6291460
  425.3 4.9 copy-start.20
  425.3 4.9 copy-start.22
  428.1 24.7 %collective-permute-start.3 = (bf16[4,256,512]{2,1,0:T(8,128)(2,1)S(1)}, bf16[4,256,512]{2,1,0:T(8,128)(2,1)S(1)}, u32[]{:S(2)}, u32[]{:S(2)}) collective-permute-start(bf16[4,256,512]{2,1,0:T(8,128)(2,1)S(1)} %get-tuple-element.31), channel_id=1, source_target_pairs={{0,4},{4,0},{1,5},{5,1},{2,6},{6,2},{3,7},{7,3},{8,12},{12,8},{9,1... | collective-permute-start | bytes 3145736 | tf_op jit(solution)/shard_map/ppermute | solution.py:17
  432.2 20.6 %copy-start.5 = (bf16[1024,512]{1,0:T(8,128)(2,1)S(1)}, bf16[1024,512]{1,0:T(8,128)(2,1)}, u32[]{:S(2)}) copy-start(bf16[1024,512]{1,0:T(8,128)(2,1)} %param.5) | copy-start | bytes 3145732
  432.2 20.6 %copy-start.9 = (bf16[4,256,512]{2,1,0:T(8,128)(2,1)S(1)}, bf16[4,256,512]{2,1,0:T(8,128)(2,1)}, u32[]{:S(2)}) copy-start(bf16[4,256,512]{2,1,0:T(8,128)(2,1)} %all_to_all.117) | copy-start | bytes 3145732
  456.7 3.0 copy-start.6
  459.7 4.5 copy-start
  465.9 3.0 copy-start.16
  468.9 12.8 %copy-start.10 = (bf16[4,256,512]{2,1,0:T(8,128)(2,1)S(1)}, bf16[4,256,512]{2,1,0:T(8,128)(2,1)}, u32[]{:S(2)}) copy-start(bf16[4,256,512]{2,1,0:T(8,128)(2,1)} %all_to_all.117) | copy-start | bytes 3145732
  (14 other events, 23.2 us)
Sparse Core Ops, SparseCore 0:
  455.1 61.3 all-reduce.2
where the time goes:
time: 528 us; the launch traced here: 527 us
  blocking collectives  297 us (56%)
  waiting for transfers between devices  117 us (22%)
  local copies, waits for them, and re-layouts  47.4 us (9%)
  other arithmetic  24.7 us (5%)
  matrix products  18.5 us (4%)
  between operations  14.4 us (3%)
  starting transfers between devices  7.9 us (1%)
    all_to_all x4, blocking collectives, to_columns(): lax.all_to_all(values, ('chan', 'bfly'), split_axis=1, concat_axis=0, til...  149 us
    all_to_all x4, blocking collectives, to_rows(): lax.all_to_all(values, ('chan', 'bfly'), split_axis=0, concat_axis=1, til...  138 us
    ppermute x4, waiting for transfers between devices, partner_2(): return lax.ppermute(block, axis, route)  85.8 us
    psum x1, waiting for transfers between devices, local(): lax.psum(all_right.astype(jnp.bfloat16), 'samp').astype(jnp.float32)  31.4 us
    convert_element_type x6, local copies, waits for them, and re-layouts, local(): activation.astype(jnp.float32)  11.5 us
    unnamed x68, local copies, waits for them, and re-layouts  11.5 us
  transfers between devices with their start and end apart: 5, of which 5 were waited for; matrix products, arithmetic and copies ran while one was open for 4% of the time, Pallas kernels for 0%

commit v1 on v0

--- a/solution.py
+++ b/solution.py
@@ -94,7 +94,7 @@
     all_left = jnp.stack(lefts)
     all_mix = jnp.stack(mixes)
     all_right, all_left, all_mix = (
-        lax.psum(all_right.astype(jnp.bfloat16), "samp").astype(jnp.float32),
+        jnp.sum(lax.all_gather(all_right.astype(jnp.bfloat16), "samp"), axis=0).astype(jnp.float32),
         lax.psum(all_left.astype(jnp.bfloat16), "samp").astype(jnp.float32),
         lax.psum(all_mix.astype(jnp.bfloat16), "samp").astype(jnp.float32),
     )

time: 528 us -> 555 us (1.051); the launches traced: 527 us -> 546 us
  waiting for transfers between devices: 117 us -> 131 us
    all_gather x0 -> x1, waiting for transfers between devices: none -> 40.7 us  [local(): lax.all_gather(all_right.astype(jnp.bfloat16), 'samp')]
    psum x1, waiting for transfers between devices: 31.4 us -> 4.94 us  [local(): lax.psum(all_left.astype(jnp.bfloat16), 'samp').astype(jnp.float32)]
    unnamed x68 -> x61, local copies, waits for them, and re-layouts: 11.5 us -> 8.6 us
  transfers between devices with their start and end apart: 5 -> 6, of which waited for: 5 -> 6; matrix products, arithmetic and copies ran while one was open for 4% -> 6% of each run, Pallas kernels for 0% -> 0%
where the time goes in v1:
time: 555 us; the launch traced here: 546 us
  blocking collectives  296 us (53%)
  waiting for transfers between devices  131 us (24%)
  local copies, waits for them, and re-layouts  46.8 us (8%)
  other arithmetic  28.9 us (5%)
  matrix products  21.3 us (4%)
  between operations  14.6 us (3%)
  starting transfers between devices  7.84 us (1%)
    all_to_all x4, blocking collectives, to_columns(): lax.all_to_all(values, ('chan', 'bfly'), split_axis=1, concat_axis=0, til...  149 us
    all_to_all x4, blocking collectives, to_rows(): lax.all_to_all(values, ('chan', 'bfly'), split_axis=0, concat_axis=1, til...  138 us
    ppermute x4, waiting for transfers between devices, partner_2(): return lax.ppermute(block, axis, route)  85 us
    all_gather x1, waiting for transfers between devices, local(): lax.all_gather(all_right.astype(jnp.bfloat16), 'samp')  40.7 us
    convert_element_type x6, local copies, waits for them, and re-layouts, local(): activation.astype(jnp.float32)  11.5 us
  transfers between devices with their start and end apart: 6, of which 6 were waited for; matrix products, arithmetic and copies ran while one was open for 6% of the time, Pallas kernels for 0%

profile of v1, /device:TPU:1, one launch (start us, length us, event | category | flops | bytes accessed | tf_op | source)
XLA Modules:
  0.0 546.2 jit_solution(501467097224047496)
XLA Ops:
  11.2 21.5 %collective-permute-done = bf16[4,256,512]{2,1,0:T(8,128)(2,1)S(1)} collective-permute-done((bf16[4,256,512]{2,1,0:T(8,128)(2,1)S(1)}, bf16[4,256,512]{2,1,0:T(8,128)(2,1)S(1)}, u32[]{:S(2)}, u32[]{:S(2)}) %collective-permute-start) | collective-permute-done | bytes 1048608 | tf_op jit(solution)/shard_map/ppermute | solution.py:17
  34.6 43.4 %all_to_all.126 = bf16[4,256,512]{2,0,1:T(4,128)(2,1)S(1)} all-to-all(bf16[4,256,512]{2,0,1:T(4,128)(2,1)S(1)} %copy.89), channel_id=1, replica_groups=mesh['chan'=32,'bfly'=2,'samp'=4] {'chan','bfly'}, dimensions={1} | all-to-all | bytes 2097152 | tf_op jit(solution)/shard_map/all_to_all | solution.py:21
  82.0 34.5 %all_to_all.127 = bf16[256,4,512]{2,1,0:T(4,128)(2,1)S(1)} all-to-all(bf16[256,4,512]{2,1,0:T(4,128)(2,1)S(1)} %copy.92), channel_id=1, replica_groups=mesh['chan'=32,'bfly'=2,'samp'=4] {'chan','bfly'}, dimensions={0} | all-to-all | bytes 2097152 | tf_op jit(solution)/shard_map/all_to_all | solution.py:25
  123.6 22.6 %collective-permute-done.1 = bf16[4,256,512]{1,2,0:T(8,128)(2,1)S(1)} collective-permute-done((bf16[4,256,512]{1,2,0:T(8,128)(2,1)S(1)}, bf16[4,256,512]{1,2,0:T(8,128)(2,1)S(1)}, u32[]{:S(2)}, u32[]{:S(2)}) %collective-permute-start.1) | collective-permute-done | bytes 1048608 | tf_op jit(solution)/shard_map/ppermute | solution.py:17
  151.2 36.0 %all_to_all.128 = bf16[4,256,512]{2,0,1:T(4,128)(2,1)S(1)} all-to-all(bf16[4,256,512]{2,0,1:T(4,128)(2,1)} %copy.96), channel_id=1, replica_groups=mesh['chan'=32,'bfly'=2,'samp'=4] {'chan','bfly'}, dimensions={1} | all-to-all | bytes 2097152 | tf_op jit(solution)/shard_map/all_to_all | solution.py:21
  193.0 34.7 %all_to_all.129 = bf16[256,4,512]{2,1,0:T(4,128)(2,1)S(1)} all-to-all(bf16[256,4,512]{2,1,0:T(4,128)(2,1)} %copy.99), channel_id=1, replica_groups=mesh['chan'=32,'bfly'=2,'samp'=4] {'chan','bfly'}, dimensions={0} | all-to-all | bytes 2097152 | tf_op jit(solution)/shard_map/all_to_all | solution.py:25
  229.7 2.9 reshape.81
  232.6 2.7 fusion.13
  236.2 34.6 %all_to_all.130 = bf16[4,256,512]{2,0,1:T(4,128)(2,1)S(1)} all-to-all(bf16[4,256,512]{2,0,1:T(4,128)(2,1)S(1)} %copy.102), channel_id=1, replica_groups=mesh['chan'=32,'bfly'=2,'samp'=4] {'chan','bfly'}, dimensions={1} | all-to-all | bytes 2097152 | tf_op jit(solution)/shard_map/all_to_all | solution.py:21
  276.4 34.7 %all_to_all.131 = bf16[256,4,512]{2,1,0:T(4,128)(2,1)S(1)} all-to-all(bf16[256,4,512]{2,1,0:T(4,128)(2,1)} %copy.105), channel_id=1, replica_groups=mesh['chan'=32,'bfly'=2,'samp'=4] {'chan','bfly'}, dimensions={0} | all-to-all | bytes 2097152 | tf_op jit(solution)/shard_map/all_to_all | solution.py:25
  318.5 22.6 %collective-permute-done.2 = bf16[4,256,512]{1,2,0:T(8,128)(2,1)S(1)} collective-permute-done((bf16[4,256,512]{1,2,0:T(8,128)(2,1)S(1)}, bf16[4,256,512]{1,2,0:T(8,128)(2,1)S(1)}, u32[]{:S(2)}, u32[]{:S(2)}) %collective-permute-start.2) | collective-permute-done | bytes 1048608 | tf_op jit(solution)/shard_map/ppermute | solution.py:17
  341.2 4.5 fusion.10
  346.5 35.4 %all_to_all.132 = bf16[4,256,512]{2,0,1:T(4,128)(2,1)S(1)} all-to-all(bf16[4,256,512]{2,0,1:T(4,128)(2,1)S(1)} %copy.109), channel_id=1, replica_groups=mesh['chan'=32,'bfly'=2,'samp'=4] {'chan','bfly'}, dimensions={1} | all-to-all | bytes 2097152 | tf_op jit(solution)/shard_map/all_to_all | solution.py:21
  387.6 34.7 %all_to_all.133 = bf16[256,4,512]{2,1,0:T(4,128)(2,1)S(1)} all-to-all(bf16[256,4,512]{2,1,0:T(4,128)(2,1)} %copy.112), channel_id=1, replica_groups=mesh['chan'=32,'bfly'=2,'samp'=4] {'chan','bfly'}, dimensions={0} | all-to-all | bytes 2097152 | tf_op jit(solution)/shard_map/all_to_all | solution.py:25
  425.8 3.3 fusion.18
  435.9 18.2 %collective-permute-done.3 = bf16[4,256,512]{2,1,0:T(8,128)(2,1)} collective-permute-done((bf16[4,256,512]{2,1,0:T(8,128)(2,1)}, bf16[4,256,512]{2,1,0:T(8,128)(2,1)}, u32[]{:S(2)}, u32[]{:S(2)}) %collective-permute-start.3) | collective-permute-done | bytes 1048608 | tf_op jit(solution)/shard_map/ppermute | solution.py:17
  461.0 3.0 reshape.79
  464.0 4.5 add_convert_fusion
  473.9 4.9 all-reduce.2.cloned.1.call-done
  478.9 2.7 convert_element_type.234
  481.6 8.1 %psum.15 = bf16[2,2,4,256]{3,2,1,0:T(4,128)(2,1)S(1)} all-reduce(bf16[2,2,4,256]{3,2,1,0:T(4,128)(2,1)S(1)} %pad_maximum_fusion.2), channel_id=1, replica_groups=mesh['chan'=32,'bfly'=2,'samp'=4] {'samp'}, use_global_device_ids=true, to_apply=%region_2.3 | all-reduce | flops 4096 | bytes 16384 | tf_op jit(solution)/shard_map/psum | solution.py:99
  490.4 2.9 fusion.11
  493.2 40.7 %all-gather.2.cloned.1.call-done = bf16[4,2,4,256,256]{4,3,2,1,0:T(8,128)(2,1)} async-done(((bf16[1,2,4,256,256]{4,3,2,1,0:T(8,128)(2,1)}), bf16[4,2,4,256,256]{4,3,2,1,0:T(8,128)(2,1)}) %all-gather.2.cloned.1.call-update) | async-done | bytes 4194320 | tf_op jit(solution)/shard_map/all_gather | solution.py:97
  534.0 3.0 reduce_sum.12
  (114 shorter events, 75.3 us)
Async XLA Ops:
  7.2 4.1 copy-start.28
  7.2 471.7 %all-reduce.2.cloned.1.call-start = ((), (), s32[]{:S(2)}) async-start(), calls=%async_computation.9 | async-start | bytes 2097152 | tf_op jit(solution)/shard_map/psum | solution.py:98
  9.1 25.5 %copy-start.1 = (bf16[4,256,512]{2,1,0:T(8,128)(2,1)}, bf16[4,256,512]{2,1,0:T(8,128)(2,1)S(1)}, u32[]{:S(2)}) copy-start(bf16[4,256,512]{2,1,0:T(8,128)(2,1)S(1)} %convolution_convert_fusion.5) | copy-start | bytes 3145732
  9.1 23.7 %collective-permute-start = (bf16[4,256,512]{2,1,0:T(8,128)(2,1)S(1)}, bf16[4,256,512]{2,1,0:T(8,128)(2,1)S(1)}, u32[]{:S(2)}, u32[]{:S(2)}) collective-permute-start(bf16[4,256,512]{2,1,0:T(8,128)(2,1)S(1)} %convolution_convert_fusion.5), channel_id=1, source_target_pairs={{0,4},{4,0},{1,5},{5,1},{2,6},{6,2},{3,7},{7,3},{8,12},{12,8},{9,1... | collective-permute-start | bytes 3145736 | tf_op jit(solution)/shard_map/ppermute | solution.py:17
  34.6 44.0 %copy-start.9 = (f32[2,4,256,256]{3,2,1,0:T(8,128)S(1)}, f32[2,4,256,256]{3,2,1,0:T(8,128)}, u32[]{:S(2)}) copy-start(f32[2,4,256,256]{3,2,1,0:T(8,128)} %param.8) | copy-start | bytes 6291460
  121.3 24.9 %copy-start.6 = (bf16[4,256,512]{2,1,0:T(8,128)(2,1)}, bf16[4,256,512]{2,1,0:T(8,128)(2,1)S(1)}, u32[]{:S(2)}) copy-start(bf16[4,256,512]{2,1,0:T(8,128)(2,1)S(1)} %add_convert_fusion.1) | copy-start | bytes 3145732
  121.9 24.4 %collective-permute-start.1 = (bf16[4,256,512]{1,2,0:T(8,128)(2,1)S(1)}, bf16[4,256,512]{1,2,0:T(8,128)(2,1)S(1)}, u32[]{:S(2)}, u32[]{:S(2)}) collective-permute-start(bf16[4,256,512]{1,2,0:T(8,128)(2,1)S(1)} %fusion.24), channel_id=1, source_target_pairs={{0,4},{4,0},{1,5},{5,1},{2,6},{6,2},{3,7},{7,3},{8,12},{12,8},{9,1... | collective-permute-start | bytes 3145736 | tf_op jit(solution)/shard_map/ppermute | solution.py:17
  151.2 37.6 %copy-start.10 = (f32[2,4,256,256]{3,2,1,0:T(8,128)S(1)}, f32[2,4,256,256]{3,2,1,0:T(8,128)}, u32[]{:S(2)}) copy-start(f32[2,4,256,256]{3,2,1,0:T(8,128)} %param.8) | copy-start | bytes 6291460
  236.2 36.1 %copy-start.11 = (f32[2,4,256,256]{3,2,1,0:T(8,128)S(1)}, f32[2,4,256,256]{3,2,1,0:T(8,128)}, u32[]{:S(2)}) copy-start(f32[2,4,256,256]{3,2,1,0:T(8,128)} %param.8) | copy-start | bytes 6291460
  315.0 26.1 %copy-start.2 = (bf16[4,256,512]{1,2,0:T(8,128)(2,1)S(1)}, bf16[4,256,512]{1,2,0:T(8,128)(2,1)}, u32[]{:S(2)}) copy-start(bf16[4,256,512]{1,2,0:T(8,128)(2,1)} %copy.107) | copy-start | bytes 3145732
  315.0 26.1 %copy-start.24 = (bf16[2,4,256,256]{3,2,1,0:T(8,128)(2,1)S(1)}, bf16[2,4,256,256]{3,2,1,0:T(8,128)(2,1)}, u32[]{:S(2)}) copy-start(bf16[2,4,256,256]{3,2,1,0:T(8,128)(2,1)} %param.7) | copy-start | bytes 3145732
  316.6 24.6 %collective-permute-start.2 = (bf16[4,256,512]{1,2,0:T(8,128)(2,1)S(1)}, bf16[4,256,512]{1,2,0:T(8,128)(2,1)S(1)}, u32[]{:S(2)}, u32[]{:S(2)}) collective-permute-start(bf16[4,256,512]{1,2,0:T(8,128)(2,1)S(1)} %fusion.8), channel_id=1, source_target_pairs={{0,4},{4,0},{1,5},{5,1},{2,6},{6,2},{3,7},{7,3},{8,12},{12,8},{9,1... | collective-permute-start | bytes 3145736 | tf_op jit(solution)/shard_map/ppermute | solution.py:17
  341.2 4.5 copy-start.27
  346.5 36.9 %copy-start.12 = (f32[2,4,256,256]{3,2,1,0:T(8,128)S(1)}, f32[2,4,256,256]{3,2,1,0:T(8,128)}, u32[]{:S(2)}) copy-start(f32[2,4,256,256]{3,2,1,0:T(8,128)} %param.8) | copy-start | bytes 6291460
  425.8 5.1 copy-start.17
  425.8 5.1 copy-start.19
  429.1 25.0 %collective-permute-start.3 = (bf16[4,256,512]{2,1,0:T(8,128)(2,1)}, bf16[4,256,512]{2,1,0:T(8,128)(2,1)}, u32[]{:S(2)}, u32[]{:S(2)}) collective-permute-start(bf16[4,256,512]{2,1,0:T(8,128)(2,1)} %get-tuple-element.14), channel_id=1, source_target_pairs={{0,4},{4,0},{1,5},{5,1},{2,6},{6,2},{3,7},{7,3},{8,12},{12,8},{9,1... | collective-permute-start | bytes 3145736 | tf_op jit(solution)/shard_map/ppermute | solution.py:17
  433.0 101.0 %all-gather.2.cloned.1.call-start = ((), (), s32[]{:S(2)}) async-start(), calls=%async_computation.8 | async-start | bytes 5242880 | tf_op jit(solution)/shard_map/all_gather | solution.py:97
  433.3 20.8 %copy-start.4 = (bf16[1024,512]{1,0:T(8,128)(2,1)S(1)}, bf16[1024,512]{1,0:T(8,128)(2,1)}, u32[]{:S(2)}) copy-start(bf16[1024,512]{1,0:T(8,128)(2,1)} %param.5) | copy-start | bytes 3145732
  433.3 20.8 %copy-start.7 = (bf16[4,256,512]{2,1,0:T(8,128)(2,1)S(1)}, bf16[4,256,512]{2,1,0:T(8,128)(2,1)}, u32[]{:S(2)}) copy-start(bf16[4,256,512]{2,1,0:T(8,128)(2,1)} %all_to_all.117) | copy-start | bytes 3145732
  464.0 4.5 copy-start
  473.9 16.5 %copy-start.8 = (bf16[4,256,512]{2,1,0:T(8,128)(2,1)S(1)}, bf16[4,256,512]{2,1,0:T(8,128)(2,1)}, u32[]{:S(2)}) copy-start(bf16[4,256,512]{2,1,0:T(8,128)(2,1)} %all_to_all.117) | copy-start | bytes 3145732
  473.9 16.5 %copy-start.25 = (bf16[2,4,256,256]{3,2,1,0:T(8,128)(2,1)S(1)}, bf16[2,4,256,256]{3,2,1,0:T(8,128)(2,1)}, u32[]{:S(2)}) copy-start(bf16[2,4,256,256]{3,2,1,0:T(8,128)(2,1)} %param.7) | copy-start | bytes 3145732
  473.9 16.4 %copy-start.26 = (bf16[4,256,512]{2,1,0:T(8,128)(2,1)S(1)}, bf16[4,256,512]{2,1,0:T(8,128)(2,1)}, u32[]{:S(2)}) copy-start(bf16[4,256,512]{2,1,0:T(8,128)(2,1)} %get-tuple-element.20) | copy-start | bytes 3145732
  (11 other events, 20.0 us)
Sparse Core Ops, SparseCore 0:
  433.1 45.6 all-reduce.1
  480.8 53.1 all-gather.1
